TPU v7x, 256 devices: a whole 4x4x8 slice. The times are simulated.
256 devices in a mesh: row: 16 (over y, x), col: 16 (over z, core).
Axes of the slice: x: 4, y: 4, z: 8, core: 2. Of those that a mesh axis runs over, the one named last changes fastest.
Arguments:
- targets: float32 [2, 131072], P(None, ('row', 'col')), may hold values from 0 to 1
- sources: bfloat16 [2, 32768], P(None, 'col'), may hold values from 0 to 1
- omega: bfloat16 [256, 32768], P(None, 'col'), may hold values from -0.03125 to 0.03125
- tree_order: int32 [131072], P(('row', 'col')), may hold values from 0 to 131071, each once
- leaf_pivots: int32 [256, 128], P(('row', 'col')), may hold values from 0 to 511, all different within a row
- pivots_one: int32 [128, 128], replicated, may hold values from 0 to 255, all different within a row
- pivots_two: int32 [64, 128], replicated, may hold values from 0 to 255, all different within a row
- pivots_three: int32 [32, 128], replicated, may hold values from 0 to 255, all different within a row
Outputs:
- leaf_interp: float32 [131072, 128], P(('row', 'col'))
- level_one_interp: float32 [32768, 128], P(('row', 'col'))
- level_two_interp: float32 [16384, 128], P(('row', 'col'))
- level_three_interp: float32 [8192, 128], P(('row', 'col'))
- root_sketch: float32 [4096, 256], P(('row', 'col'))
Inputs may be any that keep to these rules, and one draw needn't show every extreme that they name: tree_order names every target point once. `leaf_pivots`: each row names 128 distinct positions. `pivots_one`: each row names 128 distinct positions. `pivots_two`: each row names 128 distinct positions. `pivots_three`: each row names 128 distinct positions.
All inputs are finite; a program needn't handle non-finite values.
Results may differ from a plain program's by a relative error of at most 0.0074.
Values may be sent and summed in bfloat16 or wider, within the bound.
No kernel may reach another device: no remote copies, remote signals or barrier semaphores. Data moves between devices by JAX's collectives and lax.ppermute only.
A program may use at most 192 MiB of HBM per device.

v0:
```python
import math
import jax
import jax.numpy as jnp
from jax import lax
from jax.sharding import Mesh
from jax.sharding import PartitionSpec as P

LEAF = 512
S = 256
LEVELS = 3
ROW_COL = ("row_0", "row_1", "col_0", "col_1")
COL = ("col_0", "col_1")
ROW = ("row_0", "row_1")
RIDGE = 0.1
DELTA_SQUARED = 0.0001


def copy_for_each(value, axis):
    copies = jnp.broadcast_to(value, (lax.axis_size(axis), *value.shape))
    return lax.all_to_all(copies, axis, split_axis=0, concat_axis=0, tiled=True)


def laid_out(parts, dim):
    parts = jnp.moveaxis(parts, 0, dim)
    shape = parts.shape
    return parts.reshape(*shape[:dim], shape[dim] * shape[dim + 1], *shape[dim + 2 :])


def gathered_by_axis(value, axes, dim):
    far, near = axes
    parts = copy_for_each(copy_for_each(value, far), near)
    return laid_out(parts.swapaxes(0, 1).reshape(-1, *value.shape), dim)


def partner_2(block, axis, stride):
    count = lax.axis_size(axis)
    route = []
    for low in range(count):
        high = low | 1 << stride
        if high != low and high < count:
            route += [(low, high), (high, low)]
    return lax.ppermute(block, axis, route)


def kernel_block(points, source_pts):
    delta_x = points[0][:, None] - source_pts[0][None, :].astype(jnp.float32)
    delta_y = points[1][:, None] - source_pts[1][None, :].astype(jnp.float32)
    return (-0.5 * jnp.log(delta_x * delta_x + delta_y * delta_y + DELTA_SQUARED)).astype(
        jnp.bfloat16
    )


def select_factor(candidates, pivots):
    chosen = jnp.take(candidates, pivots, axis=0)
    gram_matrix = jnp.dot(chosen, chosen.T, precision=lax.Precision.HIGHEST)
    ridge_shift = RIDGE * (jnp.trace(gram_matrix) / chosen.shape[0] + 1e-06)
    shifted = gram_matrix + ridge_shift * jnp.eye(chosen.shape[0], dtype=gram_matrix.dtype)
    return (chosen, jnp.linalg.cholesky(shifted))


def solve_rows(chosen, factor, row_block):
    right_side = jnp.dot(chosen, row_block.T, precision=lax.Precision.HIGHEST)
    first = lax.linalg.triangular_solve(factor, right_side, left_side=True, lower=True)
    second = lax.linalg.triangular_solve(
        factor, first, left_side=True, lower=True, transpose_a=True
    )
    return second.T


def sketch_product(points, source_pts, weights):
    panel = kernel_block(points, source_pts)
    return lax.dot_general(
        panel, weights, (((1,), (1,)), ((), ())), preferred_element_type=jnp.float32
    )


def body(targets, sources, omega, tree_order, leaf_pivots, pivots_one, pivots_two, pivots_three):
    everyone = gathered_by_axis(targets, ("row_0", ("row_1", "col_0", "col_1")), 1)
    col_count = lax.axis_size(COL)
    col_index = lax.axis_index(COL)
    row_index = lax.axis_index(ROW)
    global_index = row_index * col_count + col_index
    own_points = jnp.take(everyone, tree_order, axis=1)
    initial = jnp.zeros((LEAF, S), jnp.float32)
    running = initial
    pieces = (
        lax.all_gather(sources, COL, axis=1, tiled=True),
        lax.all_gather(omega, COL, axis=1, tiled=True),
    )
    width = pieces[0].shape[1]
    block_len = math.gcd(width, 1024)
    source_blocks = pieces[0].reshape(2, width // block_len, block_len).transpose(1, 0, 2)
    weight_blocks = pieces[1].reshape(S, width // block_len, block_len).transpose(1, 0, 2)

    def add_block(carried, items):
        return (carried + sketch_product(own_points, items[0], items[1]), None)

    running, unused = lax.scan(add_block, running, (source_blocks, weight_blocks))
    chosen, factor = select_factor(running, leaf_pivots[0])
    results = [solve_rows(chosen, factor, running)]
    tables = (pivots_one, pivots_two, pivots_three)
    for section in range(LEVELS):
        partner = partner_2(chosen, COL, section)
        high_half = col_index >> section & 1 == 1
        candidates = jnp.where(
            high_half, jnp.concatenate([partner, chosen], 0), jnp.concatenate([chosen, partner], 0)
        )
        node_index = global_index >> section + 1
        node_pivots = lax.dynamic_index_in_dim(tables[section], node_index, 0, keepdims=False)
        group_size = 2 ** (section + 1)
        share_rows = candidates.shape[0] // group_size
        my_rows = lax.dynamic_slice_in_dim(
            candidates, col_index % group_size * share_rows, share_rows, 0
        )
        chosen, factor = select_factor(candidates, node_pivots)
        results.append(solve_rows(chosen, factor, my_rows))
    root_rows = chosen.shape[0] // 2**LEVELS
    root_share = lax.dynamic_slice_in_dim(chosen, col_index % 2**LEVELS * root_rows, root_rows, 0)
    return (results[0], results[1], results[2], results[3], root_share)


def solution(mesh):
    finer = Mesh(mesh.devices.reshape(4, 4, 8, 2), ("row_0", "row_1", "col_0", "col_1"))
    placed = (
        P(None, ROW_COL),
        P(None, COL),
        P(None, COL),
        P(ROW_COL),
        P(ROW_COL, None),
        P(),
        P(),
        P(),
    )
    return jax.shard_map(
        body,
        mesh=finer,
        in_specs=placed,
        out_specs=(
            P(ROW_COL, None),
            P(ROW_COL, None),
            P(ROW_COL, None),
            P(ROW_COL, None),
            P(ROW_COL, None),
        ),
        check_vma=False,
    )
```

profile of v0, /device:TPU:1, one launch (start us, length us, event | category | flops | bytes accessed | tf_op | source)
XLA Modules:
  0.0 315.8 jit_solution(11301371426663765097)
XLA Ops:
  7.2 2.3 copy.50
  9.6 9.0 %all_to_all.10 = f32[4,2,512]{2,1,0:T(2,128)S(1)} all-to-all(f32[4,2,512]{2,1,0:T(2,128)S(1)} %broadcast_in_dim.51), channel_id=1, replica_groups=mesh['row_0'=4,'row_1'=4,'col_0'=8,'col_1'=2] {'row_0'}, dimensions={0} | all-to-all | bytes 32768 | tf_op jit(solution)/shard_map/all_to_all | solution.py:20
  19.8 13.6 %all-to-all-start.1 = ((f32[64,4,2,512]{3,1,2,0:T(4,128)}), f32[64,4,2,512]{3,1,2,0:T(4,128)S(1)}, u32[]{:S(2)}, u32[]{:S(2)}) async-start(f32[64,4,2,512]{3,1,2,0:T(4,128)} %broadcast_in_dim.52), calls=%async_computation.1 | async-start | bytes 2097152 | tf_op jit(solution)/shard_map/all_to_all | solution.py:20
  33.5 48.8 %all_gather.6 = bf16[2,32768]{1,0:T(2,128)(2,1)S(1)} all-gather(bf16[2,2048]{1,0:T(2,128)(2,1)S(1)} %copy-done), channel_id=1, replica_groups=mesh['row_0'=4,'row_1'=4,'col_0'=8,'col_1'=2] {'col_0','col_1'}, dimensions={1}, use_global_device_ids=true | all-gather | bytes 139264 | tf_op jit(solution)/shard_map/all_gather | solution.py:87
  84.6 30.6 %copy.61 = f32[64,4,2,512]{2,3,0,1:T(8,128)} copy(f32[64,4,2,512]{3,1,2,0:T(4,128)S(1)} %all-to-all-done.1) | data formatting | bytes 2097152 | tf_op jit(solution)/shard_map/transpose | solution.py:24
  115.2 3.6 %gather_fusion = f32[512,2]{1,0:T(8,128)S(1)} fusion(f32[2,131072]{0,1:T(8,128)} %bitcast.5, s32[1024]{0:T(1024)S(1)} %pad_clamp_fusion.4), kind=kCustom, calls=%fused_computation.3 | custom fusion | bytes 10240 | tf_op jit(solution)/shard_map/jit(_take)/gather | solution.py:83
  119.1 13.6 %all-gather.2.cloned.1.call-done = bf16[256,32768]{0,1:T(8,128)(2,1)} async-done(((bf16[256,2048]{0,1:T(8,128)(2,1)}), bf16[256,32768]{0,1:T(8,128)(2,1)}) %all-gather.2.cloned.1.call-update) | async-done | bytes 16777232 | tf_op jit(solution)/shard_map/all_gather | solution.py:88
  132.7 63.3 %while.11 = (s32[]{:T(128)}, f32[512,256]{1,0:T(8,128)S(1)}, f32[2,512]{1,0:T(2,128)S(1)}, bf16[32,2,1024]{2,1,0:T(2,128)(2,1)S(1)}, bf16[32,256,1024]{1,2,0:T(8,128)(2,1)}, /*index=5*/s32[]{:T(128)}, s32[]{:T(128)}, s32[]{}) while((s32[]{:T(128)}, f32[512,256]{1,0:T(8,128)S(1)}, f32[2,512]{1,0:T(2,128)S(1)}, ...), condition=%wide.region_1.2_spmd.clone, body=%wide.region_0.1_spmd.clone.sunk | while | flops 272893952 | bytes 1606259 | solution.py:98
  134.7 1.9 convolution_add_fusion.2
  136.7 1.9 convolution_add_fusion.2
  138.7 1.9 convolution_add_fusion.2
  160.4 1.9 convolution_add_fusion.2
  162.4 1.9 convolution_add_fusion.2
  164.4 1.9 convolution_add_fusion.2
  186.2 1.9 convolution_add_fusion.2
  199.8 11.7 %cholesky.74 = f32[128,128]{1,0:T(8,128)S(1)} custom-call(f32[128,128]{1,0:T(8,128)S(1)} %copy.54), custom_call_target="Cholesky" | custom-call | tf_op jit(solution)/shard_map/jit(cholesky)/cholesky | solution.py:58
  212.8 9.8 %custom-call.22 = f32[1,128,128]{1,2,0:T(8,128)S(1)} custom-call(f32[1,128,128]{2,1,0:T(8,128)S(1)} %fusion.13), custom_call_target="InvertDiagBlocksLowerTriangular" | custom-call | tf_op jit(solution)/shard_map/triangular_solve | solution.py:64
  227.4 11.7 %cholesky.85 = f32[128,128]{1,0:T(8,128)S(1)} custom-call(f32[128,128]{1,0:T(8,128)S(1)} %copy.56), custom_call_target="Cholesky" | custom-call | tf_op jit(solution)/shard_map/jit(cholesky)/cholesky | solution.py:58
  240.4 9.8 %custom-call.23 = f32[1,128,128]{1,2,0:T(8,128)S(1)} custom-call(f32[1,128,128]{2,1,0:T(8,128)S(1)} %fusion.14), custom_call_target="InvertDiagBlocksLowerTriangular" | custom-call | tf_op jit(solution)/shard_map/triangular_solve | solution.py:64
  252.6 3.0 collective-permute-start.2
  257.4 11.7 %cholesky.96 = f32[128,128]{1,0:T(8,128)S(1)} custom-call(f32[128,128]{1,0:T(8,128)S(1)} %copy.58), custom_call_target="Cholesky" | custom-call | tf_op jit(solution)/shard_map/jit(cholesky)/cholesky | solution.py:58
  270.4 9.8 %custom-call.24 = f32[1,128,128]{1,2,0:T(8,128)S(1)} custom-call(f32[1,128,128]{2,1,0:T(8,128)S(1)} %fusion.15), custom_call_target="InvertDiagBlocksLowerTriangular" | custom-call | tf_op jit(solution)/shard_map/triangular_solve | solution.py:64
  284.2 11.7 %cholesky.107 = f32[128,128]{1,0:T(8,128)S(1)} custom-call(f32[128,128]{1,0:T(8,128)S(1)} %copy.60), custom_call_target="Cholesky" | custom-call | tf_op jit(solution)/shard_map/jit(cholesky)/cholesky | solution.py:58
  297.3 9.8 %custom-call.25 = f32[1,128,128]{1,2,0:T(8,128)S(1)} custom-call(f32[1,128,128]{2,1,0:T(8,128)S(1)} %fusion.16), custom_call_target="InvertDiagBlocksLowerTriangular" | custom-call | tf_op jit(solution)/shard_map/triangular_solve | solution.py:64
  (179 shorter events, 73.2 us)
Async XLA Ops:
  7.2 2.4 copy-start.2
  7.2 125.5 %all-gather.2.cloned.1.call-start = ((), (), s32[]{:S(2)}) async-start(), calls=%async_computation.2 | async-start | bytes 17825792 | tf_op jit(solution)/shard_map/all_gather | solution.py:88
  9.5 24.0 %copy-start = (bf16[2,2048]{1,0:T(2,128)(2,1)S(1)}, bf16[2,2048]{1,0:T(2,128)(2,1)}, u32[]{:S(2)}) copy-start(bf16[2,2048]{1,0:T(2,128)(2,1)} %param.14) | copy-start | bytes 24580
  9.5 74.9 %copy-start.1 = (s32[512]{0:T(512)S(1)}, s32[512]{0:T(512)}, u32[]{:S(2)}) copy-start(s32[512]{0:T(512)} %param.16) | copy-start | bytes 6148
  9.5 74.9 %copy-start.3 = (s32[1,128]{1,0:T(1,128)S(1)}, s32[1,128]{1,0:T(1,128)}, u32[]{:S(2)}) copy-start(s32[1,128]{1,0:T(1,128)} %param.17) | copy-start | bytes 1540
  19.8 64.7 %all-to-all-start.1 = ((f32[64,4,2,512]{3,1,2,0:T(4,128)}), f32[64,4,2,512]{3,1,2,0:T(4,128)S(1)}, u32[]{:S(2)}, u32[]{:S(2)}) async-start(f32[64,4,2,512]{3,1,2,0:T(4,128)} %broadcast_in_dim.52), calls=%async_computation.1 | async-start | bytes 2097152 | tf_op jit(solution)/shard_map/all_to_all | solution.py:20
  196.9 27.5 %collective-permute-start = (f32[128,256]{1,0:T(8,128)S(1)}, f32[128,256]{1,0:T(8,128)S(1)}, u32[]{:S(2)}, u32[]{:S(2)}) collective-permute-start(f32[128,256]{1,0:T(8,128)S(1)} %broadcast_select_fusion.3), channel_id=1, source_target_pairs={{0,1},{1,0},{2,3},{3,2},{4,5},{5,4},{6,7},{7,6},{8,9},{9,8},{10,11... | collective-permute-start | bytes 393224 | tf_op jit(solution)/shard_map/ppermute | solution.py:42
  225.3 26.5 %collective-permute-start.1 = (f32[128,256]{1,0:T(8,128)S(1)}, f32[128,256]{1,0:T(8,128)S(1)}, u32[]{:S(2)}, u32[]{:S(2)}) collective-permute-start(f32[128,256]{1,0:T(8,128)S(1)} %broadcast_select_fusion.2), channel_id=1, source_target_pairs={{0,2},{2,0},{1,3},{3,1},{4,6},{6,4},{5,7},{7,5},{8,10},{10,8},{9,1... | collective-permute-start | bytes 393224 | tf_op jit(solution)/shard_map/ppermute | solution.py:42
  252.6 28.9 %collective-permute-start.2 = (f32[128,256]{1,0:T(8,128)S(1)}, f32[128,256]{1,0:T(8,128)S(1)}, u32[]{:S(2)}, u32[]{:S(2)}) collective-permute-start(f32[128,256]{1,0:T(8,128)S(1)} %broadcast_select_fusion.1), channel_id=1, source_target_pairs={{0,4},{4,0},{1,5},{5,1},{2,6},{6,2},{3,7},{7,3},{8,12},{12,8},{9,1... | collective-permute-start | bytes 393224 | tf_op jit(solution)/shard_map/ppermute | solution.py:42
Sparse Core Ops, SparseCore 0:
  9.8 122.7 all-gather.1
where the time goes:
time: 318 us; the launch traced here: 316 us
  other arithmetic  94.7 us (30%)
  matrix products  71.2 us (22%)
  blocking collectives  57.8 us (18%)
  local copies, waits for them, and re-layouts  42.5 us (13%)
  starting transfers between devices  17.4 us (5%)
  between operations  17.2 us (5%)
  waiting for transfers between devices  13.6 us (4%)
    dot_general x32, matrix products, sketch_product(): lax.dot_general(panel, weights, (((1,), (1,)), ((), ())), preferred_eleme...  61.3 us
    another operation x12, other arithmetic, select_factor(): return (chosen, jnp.linalg.cholesky(shifted))  49.6 us
    all_gather x1, blocking collectives, body(): lax.all_gather(sources, COL, axis=1, tiled=True)  48.8 us
    another operation x8, other arithmetic, solve_rows(): lax.linalg.triangular_solve(factor, first, left_side=True, lower=True, tr...  41.9 us
    transpose x1, local copies, waits for them, and re-layouts, laid_out(): parts = jnp.moveaxis(parts, 0, dim)  30.6 us
    all_to_all x1, starting transfers between devices, copy_for_each(): return lax.all_to_all(copies, axis, split_axis=0, concat_axis=0, tiled=True)  13.6 us
    all_gather x1, waiting for transfers between devices, body(): lax.all_gather(omega, COL, axis=1, tiled=True)  13.6 us
    all_to_all x1, blocking collectives, copy_for_each(): return lax.all_to_all(copies, axis, split_axis=0, concat_axis=0, tiled=True)  9.03 us
  transfers between devices with their start and end apart: 5, of which 1 were waited for; matrix products, arithmetic and copies ran while one was open for 36% of the time, Pallas kernels for 0%

commit v1 on v0

--- a/solution.py
+++ b/solution.py
@@ -1,3 +1,4 @@
+import functools
 import math
 import jax
 import jax.numpy as jnp
@@ -13,6 +14,21 @@
 ROW = ("row_0", "row_1")
 RIDGE = 0.1
 DELTA_SQUARED = 0.0001
+
+
+def point_array(frame_in, which_dim):
+    return jnp.concatenate(
+        lax.all_to_all(
+            jnp.stack([frame_in for _ in range(lax.axis_size(COL))]),
+            axis_name=COL,
+            split_axis=0,
+            concat_axis=0,
+        ),
+        axis=which_dim,
+    )
+
+
+trace_the_lines = functools.partial(point_array, which_dim=1)
 
 
 def copy_for_each(value, axis):
@@ -83,10 +99,7 @@
     own_points = jnp.take(everyone, tree_order, axis=1)
     initial = jnp.zeros((LEAF, S), jnp.float32)
     running = initial
-    pieces = (
-        lax.all_gather(sources, COL, axis=1, tiled=True),
-        lax.all_gather(omega, COL, axis=1, tiled=True),
-    )
+    pieces = (lax.all_gather(sources, COL, axis=1, tiled=True), trace_the_lines(omega))
     width = pieces[0].shape[1]
     block_len = math.gcd(width, 1024)
     source_blocks = pieces[0].reshape(2, width // block_len, block_len).transpose(1, 0, 2)

time: 318 us -> 653 us (2.05)
  blocking collectives: 57.8 us -> 384 us
  waiting for transfers between devices: 13.6 us -> 27.1 us
  between operations: 17.2 us -> 3.77 us
    all_gather x1, blocking collectives: 48.8 us -> 375 us  [body(): lax.all_gather(sources, COL, axis=1, tiled=True)]
    all_to_all x1, waiting for transfers between devices: 0.01 us -> 27.1 us  [copy_for_each(): return lax.all_to_all(copies, axis, split_axis=0, concat_axis=0, tiled=True)]
    all_gather x1 -> x0, waiting for transfers between devices: 13.6 us -> none  [body(): lax.all_gather(omega, COL, axis=1, tiled=True)]
  transfers between devices with their start and end apart: 5 -> 5, of which waited for: 1 -> 1; matrix products, arithmetic and copies ran while one was open for 36% -> 18% of each run, Pallas kernels for 0% -> 0%
where the time goes in v1:
time: 653 us; the launch traced here: 651 us
  blocking collectives  384 us (59%)
  other arithmetic  94.7 us (15%)
  matrix products  71.1 us (11%)
  local copies, waits for them, and re-layouts  48 us (7%)
  waiting for transfers between devices  27.1 us (4%)
  starting transfers between devices  20.6 us (3%)
    all_gather x1, blocking collectives, body(): lax.all_gather(sources, COL, axis=1, tiled=True)  375 us
    dot_general x32, matrix products, sketch_product(): lax.dot_general(panel, weights, (((1,), (1,)), ((), ())), preferred_eleme...  61.3 us
    another operation x12, other arithmetic, select_factor(): return (chosen, jnp.linalg.cholesky(shifted))  49.6 us
    another operation x8, other arithmetic, solve_rows(): lax.linalg.triangular_solve(factor, first, left_side=True, lower=True, tr...  41.9 us
    transpose x1, local copies, waits for them, and re-layouts, laid_out(): parts = jnp.moveaxis(parts, 0, dim)  30.6 us
    all_to_all x1, waiting for transfers between devices, copy_for_each(): return lax.all_to_all(copies, axis, split_axis=0, concat_axis=0, tiled=True)  27.1 us
    all_to_all x1, starting transfers between devices, copy_for_each(): return lax.all_to_all(copies, axis, split_axis=0, concat_axis=0, tiled=True)  13.6 us
  transfers between devices with their start and end apart: 5, of which 1 were waited for; matrix products, arithmetic and copies ran while one was open for 18% of the time, Pallas kernels for 0%

profile of v1, /device:TPU:1, one launch (start us, length us, event | category | flops | bytes accessed | tf_op | source)
XLA Modules:
  0.0 650.8 jit_solution(18254533050767707236)
XLA Ops:
  1.3 9.0 %all_to_all.15 = f32[4,2,512]{2,1,0:T(2,128)S(1)} all-to-all(f32[4,2,512]{2,1,0:T(2,128)S(1)} %broadcast_in_dim.51), channel_id=1, replica_groups=mesh['row_0'=4,'row_1'=4,'col_0'=8,'col_1'=2] {'row_0'}, dimensions={0} | all-to-all | bytes 32768 | tf_op jit(solution)/shard_map/all_to_all | solution.py:36
  11.6 13.6 %all-to-all-start.1 = ((f32[64,4,2,512]{3,1,2,0:T(4,128)}), f32[64,4,2,512]{3,1,2,0:T(4,128)S(1)}, u32[]{:S(2)}, u32[]{:S(2)}) async-start(f32[64,4,2,512]{3,1,2,0:T(4,128)} %broadcast_in_dim.52), calls=%async_computation.1 | async-start | bytes 2097152 | tf_op jit(solution)/shard_map/all_to_all | solution.py:36
  26.7 27.1 %all-to-all-done.1 = f32[64,4,2,512]{3,1,2,0:T(4,128)S(1)} async-done(((f32[64,4,2,512]{3,1,2,0:T(4,128)}), f32[64,4,2,512]{3,1,2,0:T(4,128)S(1)}, u32[]{:S(2)}, u32[]{:S(2)}) %all-to-all-start.1) | async-done | bytes 1048608 | tf_op jit(solution)/shard_map/all_to_all | solution.py:36
  53.7 5.9 stack.2
  59.6 5.2 all-to-all-start.2
  64.9 375.0 %all_gather.3 = bf16[2,32768]{1,0:T(2,128)(2,1)S(1)} all-gather(bf16[2,2048]{1,0:T(2,128)(2,1)S(1)} %copy-done), channel_id=1, replica_groups=mesh['row_0'=4,'row_1'=4,'col_0'=8,'col_1'=2] {'col_0','col_1'}, dimensions={1}, use_global_device_ids=true | all-gather | bytes 139264 | tf_op jit(solution)/shard_map/all_gather | solution.py:102
  442.2 30.6 %copy.61 = f32[64,4,2,512]{2,3,0,1:T(8,128)} copy(f32[64,4,2,512]{3,1,2,0:T(4,128)S(1)} %all-to-all-done.1) | data formatting | bytes 2097152 | tf_op jit(solution)/shard_map/transpose | solution.py:40
  472.8 3.5 gather_fusion
  476.6 63.3 %while.11 = (s32[]{:T(128)}, f32[512,256]{1,0:T(8,128)S(1)}, f32[2,512]{1,0:T(2,128)S(1)}, bf16[32,2,1024]{2,1,0:T(2,128)(2,1)S(1)}, bf16[32,256,1024]{1,2,0:T(8,128)(2,1)}, /*index=5*/s32[]{:T(128)}, s32[]{:T(128)}, s32[]{}) while((s32[]{:T(128)}, f32[512,256]{1,0:T(8,128)S(1)}, f32[2,512]{1,0:T(2,128)S(1)}, ...), condition=%wide.region_1.2_spmd.clone, body=%wide.region_0.1_spmd.clone.sunk | while | flops 272893952 | bytes 1606259 | solution.py:111
  476.6 1.9 convolution_add_fusion.2
  496.4 1.9 convolution_add_fusion.2
  498.4 1.9 convolution_add_fusion.2
  500.4 1.9 convolution_add_fusion.2
  522.1 1.9 convolution_add_fusion.2
  524.1 1.9 convolution_add_fusion.2
  526.1 1.9 convolution_add_fusion.2
  543.6 11.7 %cholesky.74 = f32[128,128]{1,0:T(8,128)S(1)} custom-call(f32[128,128]{1,0:T(8,128)S(1)} %copy.54), custom_call_target="Cholesky" | custom-call | tf_op jit(solution)/shard_map/jit(cholesky)/cholesky | solution.py:74
  556.7 9.8 %custom-call.22 = f32[1,128,128]{1,2,0:T(8,128)S(1)} custom-call(f32[1,128,128]{2,1,0:T(8,128)S(1)} %fusion.13), custom_call_target="InvertDiagBlocksLowerTriangular" | custom-call | tf_op jit(solution)/shard_map/triangular_solve | solution.py:80
  571.2 11.7 %cholesky.85 = f32[128,128]{1,0:T(8,128)S(1)} custom-call(f32[128,128]{1,0:T(8,128)S(1)} %copy.56), custom_call_target="Cholesky" | custom-call | tf_op jit(solution)/shard_map/jit(cholesky)/cholesky | solution.py:74
  584.2 9.8 %custom-call.23 = f32[1,128,128]{1,2,0:T(8,128)S(1)} custom-call(f32[1,128,128]{2,1,0:T(8,128)S(1)} %fusion.14), custom_call_target="InvertDiagBlocksLowerTriangular" | custom-call | tf_op jit(solution)/shard_map/triangular_solve | solution.py:80
  599.2 11.7 %cholesky.96 = f32[128,128]{1,0:T(8,128)S(1)} custom-call(f32[128,128]{1,0:T(8,128)S(1)} %copy.58), custom_call_target="Cholesky" | custom-call | tf_op jit(solution)/shard_map/jit(cholesky)/cholesky | solution.py:74
  612.3 9.8 %custom-call.24 = f32[1,128,128]{1,2,0:T(8,128)S(1)} custom-call(f32[1,128,128]{2,1,0:T(8,128)S(1)} %fusion.15), custom_call_target="InvertDiagBlocksLowerTriangular" | custom-call | tf_op jit(solution)/shard_map/triangular_solve | solution.py:80
  626.1 11.7 %cholesky.107 = f32[128,128]{1,0:T(8,128)S(1)} custom-call(f32[128,128]{1,0:T(8,128)S(1)} %copy.60), custom_call_target="Cholesky" | custom-call | tf_op jit(solution)/shard_map/jit(cholesky)/cholesky | solution.py:74
  639.1 9.8 %custom-call.25 = f32[1,128,128]{1,2,0:T(8,128)S(1)} custom-call(f32[1,128,128]{2,1,0:T(8,128)S(1)} %fusion.16), custom_call_target="InvertDiagBlocksLowerTriangular" | custom-call | tf_op jit(solution)/shard_map/triangular_solve | solution.py:80
  (177 shorter events, 76.3 us)
Async XLA Ops:
  11.6 42.1 %all-to-all-start.1 = ((f32[64,4,2,512]{3,1,2,0:T(4,128)}), f32[64,4,2,512]{3,1,2,0:T(4,128)S(1)}, u32[]{:S(2)}, u32[]{:S(2)}) async-start(f32[64,4,2,512]{3,1,2,0:T(4,128)} %broadcast_in_dim.52), calls=%async_computation.1 | async-start | bytes 2097152 | tf_op jit(solution)/shard_map/all_to_all | solution.py:36
  59.6 5.3 copy-start
  59.6 382.5 %copy-start.1 = (s32[512]{0:T(512)S(1)}, s32[512]{0:T(512)}, u32[]{:S(2)}) copy-start(s32[512]{0:T(512)} %param.16) | copy-start | bytes 6148
  59.6 382.5 %copy-start.2 = (s32[1,128]{1,0:T(1,128)S(1)}, s32[1,128]{1,0:T(1,128)}, u32[]{:S(2)}) copy-start(s32[1,128]{1,0:T(1,128)} %param.17) | copy-start | bytes 1540
  59.6 416.9 %all-to-all-start.2 = ((bf16[16,256,2048]{1,2,0:T(8,128)(2,1)}), bf16[16,256,2048]{1,2,0:T(8,128)(2,1)}, u32[]{:S(2)}, u32[]{:S(2)}) async-start(bf16[16,256,2048]{1,2,0:T(8,128)(2,1)} %stack.2), calls=%async_computation.2 | async-start | bytes 33554432 | tf_op jit(solution)/shard_map/all_to_all | solution.py:21
  540.8 27.4 %collective-permute-start = (f32[128,256]{1,0:T(8,128)S(1)}, f32[128,256]{1,0:T(8,128)S(1)}, u32[]{:S(2)}, u32[]{:S(2)}) collective-permute-start(f32[128,256]{1,0:T(8,128)S(1)} %broadcast_select_fusion.3), channel_id=1, source_target_pairs={{0,1},{1,0},{2,3},{3,2},{4,5},{5,4},{6,7},{7,6},{8,9},{9,8},{10,11... | collective-permute-start | bytes 393224 | tf_op jit(solution)/shard_map/ppermute | solution.py:58
  569.1 26.5 %collective-permute-start.1 = (f32[128,256]{1,0:T(8,128)S(1)}, f32[128,256]{1,0:T(8,128)S(1)}, u32[]{:S(2)}, u32[]{:S(2)}) collective-permute-start(f32[128,256]{1,0:T(8,128)S(1)} %broadcast_select_fusion.2), channel_id=1, source_target_pairs={{0,2},{2,0},{1,3},{3,1},{4,6},{6,4},{5,7},{7,5},{8,10},{10,8},{9,1... | collective-permute-start | bytes 393224 | tf_op jit(solution)/shard_map/ppermute | solution.py:58
  596.4 27.0 %collective-permute-start.2 = (f32[128,256]{1,0:T(8,128)S(1)}, f32[128,256]{1,0:T(8,128)S(1)}, u32[]{:S(2)}, u32[]{:S(2)}) collective-permute-start(f32[128,256]{1,0:T(8,128)S(1)} %broadcast_select_fusion.1), channel_id=1, source_target_pairs={{0,4},{4,0},{1,5},{5,1},{2,6},{6,2},{3,7},{7,3},{8,12},{12,8},{9,1... | collective-permute-start | bytes 393224 | tf_op jit(solution)/shard_map/ppermute | solution.py:58
